TPU v7x, 256 devices: a whole 4x4x8 slice. The times are simulated.
256 devices in a mesh: rep: 8 (over y, x_hi), blk: 32 (over z, x_lo, core).
Axes of the slice: x: 4 (x_hi: 2, x_lo: 2; x = x_hi * 2 + x_lo), y: 4, z: 8, core: 2. Of those that a mesh axis runs over, the one named last changes fastest.
Arguments:
- features: bfloat16 [131072, 128], P(('rep', 'blk')), may hold values from -6 to 6
- degrees: int32 [131072], P(('rep', 'blk')), may hold values from 1 to 32
- tile_weights: bfloat16 [8, 32, 320, 128, 128], P('rep', 'blk'), may hold values from 0 to 0.049804688
- tile_rows: int32 [8, 32, 320], P('rep', 'blk'), may hold values from 0 to 127, as said below
- tile_cols: int32 [8, 32, 320], P('rep', 'blk'), may hold values from 0 to 31, as said below
- tile_counts: int32 [8, 32], P('rep', 'blk'), may hold values from 1 to 320, as said below
- weight: bfloat16 [128, 256], replicated, may hold values from -0.5 to 0.5
- layer_bias: float32 [256], replicated, may hold values from -3 to 3
- upstream: bfloat16 [131072, 256], P(('rep', 'blk')), may hold values from -6 to 6
Outputs:
- hidden: bfloat16 [131072, 256], P(('rep', 'blk'))
- feature_grad: bfloat16 [131072, 128], P(('rep', 'blk'))
- weight_grad: float32 [128, 256], replicated
- bias_grad: float32 [256], replicated
Inputs may be any that keep to these rules, and one draw needn't show every extreme that they name: `tile_rows`: the first tile_counts slots of a device hold distinct tiles, ordered by row and then by column; a used row h lies in node block r * 32 + h // 4, whose index h // 4 is within 3 steps of the device's blk index around the loop of 32; unused slots hold the device's own first tile row. `tile_cols`: unused slots hold 0. `tile_counts`: at most 80 used slots of one device lie in the rows of one node block; this and the largest count are both reached by some device in every draw.
All inputs are finite; a program needn't handle non-finite values.
Results may differ from a plain program's by a relative error of at most 0.015.
Values may be sent and summed in bfloat16 or wider, within the bound.
A program may use at most 128 MiB of HBM per device.

v0:
```python
import jax
import jax.numpy as jnp
from jax import lax
from jax.sharding import PartitionSpec as P

REACH = 3


def shifted(value, axis, by):
    length = lax.axis_size(axis)
    return lax.ppermute(value, axis, [(i, (i + by) % length) for i in range(length)])


def node_scale(degrees):
    return 1.0 / jnp.sqrt(degrees.astype(jnp.float32) + 1.0)


def on_device(
    features, degrees, tile_weights, tile_rows, tile_cols, tile_counts, weight, layer_bias, upstream
):
    row_count, feat_width = features.shape
    tile_size = tile_weights.shape[-1]
    slot_total = tile_weights.shape[2]
    row_tiles = row_count // tile_size
    rep_count = lax.axis_size("rep")
    blk_count = lax.axis_size("blk")
    blk_index = lax.axis_index("blk")
    window_blocks = 2 * REACH + 1
    window_tiles = window_blocks * row_tiles
    column_tiles = rep_count * row_tiles
    slot_block = slot_total // (2 * (REACH + 1))
    block_total = slot_total // slot_block
    weights_dev = tile_weights[0, 0]
    rows_dev = tile_rows[0, 0]
    cols_dev = tile_cols[0, 0]
    count_dev = tile_counts[0, 0]
    group_index = rows_dev // row_tiles
    distance = (group_index - blk_index) % blk_count
    distance = jnp.where(distance > blk_count // 2, distance - blk_count, distance)
    window_rows = (distance + REACH) * row_tiles + rows_dev % row_tiles
    slot_ids = jnp.arange(slot_total, dtype=jnp.int32)
    slot_valid = slot_ids < count_dev
    window_seg = jnp.where(slot_valid, window_rows, window_tiles)
    column_seg = jnp.where(slot_valid, cols_dev, column_tiles)

    def tile_pass(source_tiles, gather_index, segment_index, segment_total, pattern):

        def add_block(block_id, running):
            slot_first = block_id * slot_block
            weights_part = lax.dynamic_slice_in_dim(weights_dev, slot_first, slot_block, 0)
            gather_part = lax.dynamic_slice_in_dim(gather_index, slot_first, slot_block, 0)
            segment_part = lax.dynamic_slice_in_dim(segment_index, slot_first, slot_block, 0)
            products = jnp.einsum(
                pattern, weights_part, source_tiles[gather_part], preferred_element_type=jnp.float32
            )
            return (
                running
                + jax.ops.segment_sum(products, segment_part, segment_total + 1)[:segment_total]
            )

        zero_sum = jnp.zeros((segment_total, tile_size, feat_width), jnp.float32)
        return lax.fori_loop(0, block_total, add_block, zero_sum)

    node_norm = node_scale(degrees)
    scaled = (node_norm[:, None] * features.astype(jnp.float32)).astype(jnp.bfloat16)
    source_rows = lax.all_gather(scaled, "rep", axis=0, tiled=True)
    source_tiles = source_rows.reshape(column_tiles, tile_size, feat_width)
    partial_value = tile_pass(source_tiles, cols_dev, window_seg, window_tiles, "tab,tbf->taf")
    partial_value = partial_value.reshape(window_blocks, row_count, feat_width)
    neighbor_sum = partial_value[REACH]
    for offset in range(-REACH, REACH + 1):
        if offset != 0:
            neighbor_sum = neighbor_sum + shifted(
                partial_value[offset + REACH].astype(jnp.bfloat16), "blk", offset
            ).astype(jnp.float32)
    aggregated = (node_norm[:, None] * (neighbor_sum + scaled.astype(jnp.float32))).astype(
        jnp.bfloat16
    )
    pre_act = jnp.dot(aggregated, weight, preferred_element_type=jnp.float32) + layer_bias
    hidden = jax.nn.silu(pre_act).astype(jnp.bfloat16)
    gate_sigmoid = jax.nn.sigmoid(pre_act)
    pre_grad = (
        upstream.astype(jnp.float32)
        * (gate_sigmoid + pre_act * gate_sigmoid * (1.0 - gate_sigmoid))
    ).astype(jnp.bfloat16)
    local_weight = jnp.dot(aggregated.T, pre_grad, preferred_element_type=jnp.float32)
    local_bias = jnp.sum(pre_grad.astype(jnp.float32), axis=0)
    weight_sum, bias_sum = lax.psum((local_weight, local_bias), ("rep", "blk"))
    grad_scale = (row_count * rep_count * blk_count) ** (-0.5)
    scaled_grad = (
        node_norm[:, None] * jnp.dot(pre_grad, weight.T, preferred_element_type=jnp.float32)
    ).astype(jnp.bfloat16)
    window_parts = [scaled_grad] * window_blocks
    for offset in range(-REACH, REACH + 1):
        if offset != 0:
            window_parts[offset + REACH] = shifted(scaled_grad, "blk", -offset)
    grad_tiles = jnp.stack(window_parts).reshape(window_tiles, tile_size, feat_width)
    column_part = tile_pass(grad_tiles, window_rows, column_seg, column_tiles, "tab,taf->tbf")
    column_sum = lax.psum_scatter(
        column_part.reshape(rep_count * row_count, feat_width).astype(jnp.bfloat16),
        "rep",
        scatter_dimension=0,
        tiled=True,
    ).astype(jnp.float32)
    feature_grad = (node_norm[:, None] * (column_sum + scaled_grad.astype(jnp.float32))).astype(
        jnp.bfloat16
    )
    return (hidden, feature_grad, weight_sum * grad_scale, bias_sum * grad_scale)


def solution(mesh):
    placed = (
        P(("rep", "blk"), None),
        P(("rep", "blk")),
        P("rep", "blk", None, None, None),
        P("rep", "blk", None),
        P("rep", "blk", None),
        P("rep", "blk"),
        P(),
        P(),
        P(("rep", "blk"), None),
    )
    return jax.shard_map(
        on_device,
        mesh=mesh,
        in_specs=placed,
        out_specs=(P(("rep", "blk"), None), P(("rep", "blk"), None), P(), P()),
        check_vma=False,
    )
```

profile of v0, /device:TPU:32, one launch (start us, length us, event | category | flops | bytes accessed | tf_op | source)
XLA Modules:
  0.0 557.3 jit_solution(4385618830677992955)
XLA Ops:
  11.8 53.4 %all-gather.2.cloned.1.call-done = bf16[4096,128]{1,0:T(8,128)(2,1)} async-done(((bf16[512,128]{1,0:T(8,128)(2,1)}), bf16[4096,128]{1,0:T(8,128)(2,1)}) %all-gather.2.cloned.1.call-update) | async-done | bytes 1048592 | tf_op jit(solution)/shard_map/all_gather | solution.py:66
  65.2 120.4 %while.28 = (s32[]{:T(128)}, f32[28,128,128]{2,1,0:T(8,128)}, s32[320]{0:T(512)S(1)}, bf16[320,128,128]{2,1,0:T(8,128)(2,1)}, s32[320]{0:T(512)S(1)}, /*index=5*...) while((s32[]{:T(128)}, f32[28,128,128]{2,1,0:T(8,128)}, ...), condition=%wide.region_2.3_spmd.clone, body=%wide.region_0.2_spmd.clone.sunk | while | flops 169346176 | bytes 23139612 | solution.py:62
  67.4 3.3 fusion.44
  71.0 6.5 %scatter_fusion = f32[29,128,128]{2,1,0:T(8,128)S(1)} fusion(f32[29,128,128]{2,1,0:T(8,128)S(1)} %broadcast.127, s32[40]{0:T(128)S(1)} %dynamic_slice.62, f32[40,128,128]{2,1,0:T(8,128)} %fusion.44), kind=kCustom, calls=%fused_computation.2.clone.clone.1 | custom fusion | flops 655360 | bytes 7864480 | tf_op jit(solution)/shard_map/while/body/eval_jaxpr/scatter-add | solution.py:58
  79.1 2.0 gather_fusion
  81.2 3.3 fusion.44
  84.7 6.5 %scatter_fusion = f32[29,128,128]{2,1,0:T(8,128)S(1)} fusion(f32[29,128,128]{2,1,0:T(8,128)S(1)} %broadcast.127, s32[40]{0:T(128)S(1)} %dynamic_slice.62, f32[40,128,128]{2,1,0:T(8,128)} %fusion.44), kind=kCustom, calls=%fused_computation.2.clone.clone.1 | custom fusion | flops 655360 | bytes 7864480 | tf_op jit(solution)/shard_map/while/body/eval_jaxpr/scatter-add | solution.py:58
  91.3 3.0 slice_add_fusion.4
  96.4 3.3 fusion.44
  100.0 6.5 %scatter_fusion = f32[29,128,128]{2,1,0:T(8,128)S(1)} fusion(f32[29,128,128]{2,1,0:T(8,128)S(1)} %broadcast.127, s32[40]{0:T(128)S(1)} %dynamic_slice.62, f32[40,128,128]{2,1,0:T(8,128)} %fusion.44), kind=kCustom, calls=%fused_computation.2.clone.clone.1 | custom fusion | flops 655360 | bytes 7864480 | tf_op jit(solution)/shard_map/while/body/eval_jaxpr/scatter-add | solution.py:58
  106.5 3.0 slice_add_fusion.4
  109.6 2.0 gather_fusion
  111.6 3.3 fusion.44
  115.2 6.5 %scatter_fusion = f32[29,128,128]{2,1,0:T(8,128)S(1)} fusion(f32[29,128,128]{2,1,0:T(8,128)S(1)} %broadcast.127, s32[40]{0:T(128)S(1)} %dynamic_slice.62, f32[40,128,128]{2,1,0:T(8,128)} %fusion.44), kind=kCustom, calls=%fused_computation.2.clone.clone.1 | custom fusion | flops 655360 | bytes 7864480 | tf_op jit(solution)/shard_map/while/body/eval_jaxpr/scatter-add | solution.py:58
  121.7 3.0 slice_add_fusion.4
  126.9 3.3 fusion.44
  130.4 6.5 %scatter_fusion = f32[29,128,128]{2,1,0:T(8,128)S(1)} fusion(f32[29,128,128]{2,1,0:T(8,128)S(1)} %broadcast.127, s32[40]{0:T(128)S(1)} %dynamic_slice.62, f32[40,128,128]{2,1,0:T(8,128)} %fusion.44), kind=kCustom, calls=%fused_computation.2.clone.clone.1 | custom fusion | flops 655360 | bytes 7864480 | tf_op jit(solution)/shard_map/while/body/eval_jaxpr/scatter-add | solution.py:58
  137.0 3.0 slice_add_fusion.4
  140.1 2.0 gather_fusion
  142.1 3.3 fusion.44
  145.7 6.5 %scatter_fusion = f32[29,128,128]{2,1,0:T(8,128)S(1)} fusion(f32[29,128,128]{2,1,0:T(8,128)S(1)} %broadcast.127, s32[40]{0:T(128)S(1)} %dynamic_slice.62, f32[40,128,128]{2,1,0:T(8,128)} %fusion.44), kind=kCustom, calls=%fused_computation.2.clone.clone.1 | custom fusion | flops 655360 | bytes 7864480 | tf_op jit(solution)/shard_map/while/body/eval_jaxpr/scatter-add | solution.py:58
  152.2 3.0 slice_add_fusion.4
  155.3 2.0 gather_fusion
  157.4 3.3 fusion.44
  160.9 6.5 %scatter_fusion = f32[29,128,128]{2,1,0:T(8,128)S(1)} fusion(f32[29,128,128]{2,1,0:T(8,128)S(1)} %broadcast.127, s32[40]{0:T(128)S(1)} %dynamic_slice.62, f32[40,128,128]{2,1,0:T(8,128)} %fusion.44), kind=kCustom, calls=%fused_computation.2.clone.clone.1 | custom fusion | flops 655360 | bytes 7864480 | tf_op jit(solution)/shard_map/while/body/eval_jaxpr/scatter-add | solution.py:58
  167.5 3.0 slice_add_fusion.4
  172.6 3.3 fusion.44
  176.2 6.5 %scatter_fusion = f32[29,128,128]{2,1,0:T(8,128)S(1)} fusion(f32[29,128,128]{2,1,0:T(8,128)S(1)} %broadcast.127, s32[40]{0:T(128)S(1)} %dynamic_slice.62, f32[40,128,128]{2,1,0:T(8,128)} %fusion.44), kind=kCustom, calls=%fused_computation.2.clone.clone.1 | custom fusion | flops 655360 | bytes 7864480 | tf_op jit(solution)/shard_map/while/body/eval_jaxpr/scatter-add | solution.py:58
  182.7 3.0 slice_add_fusion.4
  187.5 14.4 %copy.13 = bf16[1,1,320,128,128]{3,4,2,1,0:T(8,128)(2,1)} copy(bf16[1,1,320,128,128]{4,3,2,1,0:T(8,128)(2,1)} %bitcast.61) | data formatting | bytes 20971520 | tf_op args[2]
  204.2 2.6 collective-permute-start.2
  209.3 4.0 collective-permute-done.4
  213.3 2.2 collective-permute-done.1
  219.0 3.3 collective-permute-start.9
  223.9 5.1 collective-permute-done.6
  230.9 5.0 collective-permute-done.7
  236.2 113.0 %while.29 = (s32[]{:T(128)}, f32[32,128,128]{2,1,0:T(8,128)}, s32[320]{0:T(512)S(1)}, bf16[320,128,128]{1,2,0:T(8,128)(2,1)}, s32[320]{0:T(512)S(1)}, /*index=5*...) while((s32[]{:T(128)}, f32[32,128,128]{2,1,0:T(8,128)}, ...), condition=%wide.region_5.6_spmd.clone, body=%wide.region_3.5_spmd.clone.sunk | while | flops 169477248 | bytes 24188188 | solution.py:62
  237.2 3.3 fusion.47
  240.7 6.6 %scatter_fusion.1 = f32[33,128,128]{2,1,0:T(8,128)S(1)} fusion(f32[33,128,128]{2,1,0:T(8,128)S(1)} %broadcast.134, s32[40]{0:T(128)S(1)} %dynamic_slice.65, f32[40,128,128]{2,1,0:T(8,128)} %fusion.47), kind=kCustom, calls=%fused_computation.3.clone.clone.1 | custom fusion | flops 655360 | bytes 7864480 | tf_op jit(solution)/shard_map/while/body/eval_jaxpr/scatter-add | solution.py:58
  249.9 3.3 fusion.47
  253.5 6.6 %scatter_fusion.1 = f32[33,128,128]{2,1,0:T(8,128)S(1)} fusion(f32[33,128,128]{2,1,0:T(8,128)S(1)} %broadcast.134, s32[40]{0:T(128)S(1)} %dynamic_slice.65, f32[40,128,128]{2,1,0:T(8,128)} %fusion.47), kind=kCustom, calls=%fused_computation.3.clone.clone.1 | custom fusion | flops 655360 | bytes 7864480 | tf_op jit(solution)/shard_map/while/body/eval_jaxpr/scatter-add | solution.py:58
  260.1 3.2 slice_add_fusion.5
  264.2 3.3 fusion.47
  267.8 6.6 %scatter_fusion.1 = f32[33,128,128]{2,1,0:T(8,128)S(1)} fusion(f32[33,128,128]{2,1,0:T(8,128)S(1)} %broadcast.134, s32[40]{0:T(128)S(1)} %dynamic_slice.65, f32[40,128,128]{2,1,0:T(8,128)} %fusion.47), kind=kCustom, calls=%fused_computation.3.clone.clone.1 | custom fusion | flops 655360 | bytes 7864480 | tf_op jit(solution)/shard_map/while/body/eval_jaxpr/scatter-add | solution.py:58
  274.4 3.2 slice_add_fusion.5
  278.6 3.3 fusion.47
  282.2 6.6 %scatter_fusion.1 = f32[33,128,128]{2,1,0:T(8,128)S(1)} fusion(f32[33,128,128]{2,1,0:T(8,128)S(1)} %broadcast.134, s32[40]{0:T(128)S(1)} %dynamic_slice.65, f32[40,128,128]{2,1,0:T(8,128)} %fusion.47), kind=kCustom, calls=%fused_computation.3.clone.clone.1 | custom fusion | flops 655360 | bytes 7864480 | tf_op jit(solution)/shard_map/while/body/eval_jaxpr/scatter-add | solution.py:58
  288.7 3.2 slice_add_fusion.5
  292.9 3.3 fusion.47
  296.5 6.6 %scatter_fusion.1 = f32[33,128,128]{2,1,0:T(8,128)S(1)} fusion(f32[33,128,128]{2,1,0:T(8,128)S(1)} %broadcast.134, s32[40]{0:T(128)S(1)} %dynamic_slice.65, f32[40,128,128]{2,1,0:T(8,128)} %fusion.47), kind=kCustom, calls=%fused_computation.3.clone.clone.1 | custom fusion | flops 655360 | bytes 7864480 | tf_op jit(solution)/shard_map/while/body/eval_jaxpr/scatter-add | solution.py:58
  303.1 3.2 slice_add_fusion.5
  307.2 3.3 fusion.47
  310.8 6.6 %scatter_fusion.1 = f32[33,128,128]{2,1,0:T(8,128)S(1)} fusion(f32[33,128,128]{2,1,0:T(8,128)S(1)} %broadcast.134, s32[40]{0:T(128)S(1)} %dynamic_slice.65, f32[40,128,128]{2,1,0:T(8,128)} %fusion.47), kind=kCustom, calls=%fused_computation.3.clone.clone.1 | custom fusion | flops 655360 | bytes 7864480 | tf_op jit(solution)/shard_map/while/body/eval_jaxpr/scatter-add | solution.py:58
  317.4 3.2 slice_add_fusion.5
  321.6 3.3 fusion.47
  325.1 6.5 %scatter_fusion.1 = f32[33,128,128]{2,1,0:T(8,128)S(1)} fusion(f32[33,128,128]{2,1,0:T(8,128)S(1)} %broadcast.134, s32[40]{0:T(128)S(1)} %dynamic_slice.65, f32[40,128,128]{2,1,0:T(8,128)} %fusion.47), kind=kCustom, calls=%fused_computation.3.clone.clone.1 | custom fusion | flops 655360 | bytes 7864480 | tf_op jit(solution)/shard_map/while/body/eval_jaxpr/scatter-add | solution.py:58
  331.7 3.2 slice_add_fusion.5
  335.8 3.3 fusion.47
  339.4 6.5 %scatter_fusion.1 = f32[33,128,128]{2,1,0:T(8,128)S(1)} fusion(f32[33,128,128]{2,1,0:T(8,128)S(1)} %broadcast.134, s32[40]{0:T(128)S(1)} %dynamic_slice.65, f32[40,128,128]{2,1,0:T(8,128)} %fusion.47), kind=kCustom, calls=%fused_computation.3.clone.clone.1 | custom fusion | flops 655360 | bytes 7864480 | tf_op jit(solution)/shard_map/while/body/eval_jaxpr/scatter-add | solution.py:58
  346.0 3.2 slice_add_fusion.5
  349.2 2.7 convert_element_type.108
  351.9 75.9 %psum.15 = f32[256]{0:T(256)S(1)} all-reduce(f32[256]{0:T(256)S(1)} %get-tuple-element.296), channel_id=1, replica_groups=mesh['rep'=8,'blk'=32] {'rep','blk'}, use_global_device_ids=true, to_apply=%region_9.10 | all-reduce | flops 256 | bytes 2048 | tf_op jit(solution)/shard_map/psum | solution.py:88
  428.4 41.1 %all-reduce.2.cloned.1.call-done = f32[128,256]{1,0:T(8,128)} async-done(((f32[128,256]{1,0:T(8,128)}), f32[128,256]{1,0:T(8,128)}) %all-reduce.2.cloned.1.call-update) | async-done | bytes 131088 | tf_op jit(solution)/shard_map/psum | solution.py:88
  471.1 77.9 %reduce-scatter.2.cloned.1.call-done = bf16[512,128]{1,0:T(8,128)(2,1)} async-done(((bf16[4096,128]{1,0:T(8,128)(2,1)}), bf16[512,128]{1,0:T(8,128)(2,1)}) %reduce-scatter.2.cloned.1.call-update) | async-done | bytes 131088 | tf_op jit(solution)/shard_map/reduce_scatter | solution.py:99
  (135 shorter events, 45.0 us)
Async XLA Ops:
  7.2 208.5 %copy-start = (bf16[128,256]{1,0:T(8,128)(2,1)S(1)}, bf16[128,256]{1,0:T(8,128)(2,1)}, u32[]{:S(2)}) copy-start(bf16[128,256]{1,0:T(8,128)(2,1)} %param.19) | copy-start | bytes 196612
  7.2 58.0 %all-gather.2.cloned.1.call-start = ((), (), s32[]{:S(2)}) async-start(), calls=%async_computation.1 | async-start | bytes 1179648 | tf_op jit(solution)/shard_map/all_gather | solution.py:66
  9.6 459.9 %all-reduce.2.cloned.1.call-start = ((), (), s32[]{:S(2)}) async-start(), calls=%async_computation.3 | async-start | bytes 262144 | tf_op jit(solution)/shard_map/psum | solution.py:88
  187.4 19.5 %collective-permute-start.5 = (bf16[512,128]{1,0:T(8,128)(2,1)S(1)}, bf16[512,128]{1,0:T(8,128)(2,1)S(1)}, u32[]{:S(2)}, u32[]{:S(2)}) collective-permute-start(bf16[512,128]{1,0:T(8,128)(2,1)S(1)} %bitcast.69), channel_id=1, source_target_pairs={{0,3},{1,4},{2,5},{3,6},{4,7},{5,8},{6,9},{7,10},{8,11},{9,12},{10... | collective-permute-start | bytes 393224 | tf_op jit(solution)/shard_map/ppermute | solution.py:11
  187.5 28.0 %copy-start.1 = (bf16[512,128]{1,0:T(8,128)(2,1)S(1)}, bf16[512,128]{1,0:T(8,128)(2,1)}, u32[]{:S(2)}) copy-start(bf16[512,128]{1,0:T(8,128)(2,1)} %param.13) | copy-start | bytes 393220
  187.5 28.2 %copy-start.2 = (bf16[512,256]{1,0:T(8,128)(2,1)S(1)}, bf16[512,256]{1,0:T(8,128)(2,1)}, u32[]{:S(2)}) copy-start(bf16[512,256]{1,0:T(8,128)(2,1)} %param.21) | copy-start | bytes 786436
  187.5 28.2 %copy-start.3 = (f32[256]{0:T(256)S(1)}, f32[256]{0:T(256)}, u32[]{:S(2)}) copy-start(f32[256]{0:T(256)} %param.20) | copy-start | bytes 3076
  201.9 7.3 %collective-permute-start = (bf16[512,128]{1,0:T(8,128)(2,1)S(1)}, bf16[512,128]{1,0:T(8,128)(2,1)S(1)}, u32[]{:S(2)}, u32[]{:S(2)}) collective-permute-start(bf16[512,128]{1,0:T(8,128)(2,1)S(1)} %bitcast.68), channel_id=1, source_target_pairs={{0,29},{1,30},{2,31},{3,0},{4,1},{5,2},{6,3},{7,4},{8,5},{9,6},{10... | collective-permute-start | bytes 393224 | tf_op jit(solution)/shard_map/ppermute | solution.py:11
  203.6 9.7 %collective-permute-start.4 = (bf16[512,128]{1,0:T(8,128)(2,1)S(1)}, bf16[512,128]{1,0:T(8,128)(2,1)S(1)}, u32[]{:S(2)}, u32[]{:S(2)}) collective-permute-start(bf16[512,128]{1,0:T(8,128)(2,1)S(1)} %bitcast.67), channel_id=1, source_target_pairs={{0,2},{1,3},{2,4},{3,5},{4,6},{5,7},{6,8},{7,9},{8,10},{9,11},{10,... | collective-permute-start | bytes 393224 | tf_op jit(solution)/shard_map/ppermute | solution.py:11
  204.2 9.1 %collective-permute-start.3 = (bf16[512,128]{1,0:T(8,128)(2,1)S(1)}, bf16[512,128]{1,0:T(8,128)(2,1)S(1)}, u32[]{:S(2)}, u32[]{:S(2)}) collective-permute-start(bf16[512,128]{1,0:T(8,128)(2,1)S(1)} %bitcast.66), channel_id=1, source_target_pairs={{0,1},{1,2},{2,3},{3,4},{4,5},{5,6},{6,7},{7,8},{8,9},{9,10},{10,1... | collective-permute-start | bytes 393224 | tf_op jit(solution)/shard_map/ppermute | solution.py:11
  204.2 9.1 %collective-permute-start.2 = (bf16[512,128]{1,0:T(8,128)(2,1)S(1)}, bf16[512,128]{1,0:T(8,128)(2,1)S(1)}, u32[]{:S(2)}, u32[]{:S(2)}) collective-permute-start(bf16[512,128]{1,0:T(8,128)(2,1)S(1)} %bitcast.65), channel_id=1, source_target_pairs={{0,31},{1,0},{2,1},{3,2},{4,3},{5,4},{6,5},{7,6},{8,7},{9,8},{10,9... | collective-permute-start | bytes 393224 | tf_op jit(solution)/shard_map/ppermute | solution.py:11
  206.9 8.6 %collective-permute-start.1 = (bf16[512,128]{1,0:T(8,128)(2,1)S(1)}, bf16[512,128]{1,0:T(8,128)(2,1)S(1)}, u32[]{:S(2)}, u32[]{:S(2)}) collective-permute-start(bf16[512,128]{1,0:T(8,128)(2,1)S(1)} %bitcast.64), channel_id=1, source_target_pairs={{0,30},{1,31},{2,0},{3,1},{4,2},{5,3},{6,4},{7,5},{8,6},{9,7},{10,... | collective-permute-start | bytes 393224 | tf_op jit(solution)/shard_map/ppermute | solution.py:11
  217.0 19.1 %collective-permute-start.11 = (bf16[512,128]{1,0:T(8,128)(2,1)S(1)}, bf16[512,128]{1,0:T(8,128)(2,1)S(1)}, u32[]{:S(2)}, u32[]{:S(2)}) collective-permute-start(bf16[512,128]{1,0:T(8,128)(2,1)S(1)} %fusion.6), channel_id=1, source_target_pairs={{0,29},{1,30},{2,31},{3,0},{4,1},{5,2},{6,3},{7,4},{8,5},{9,6},{10... | collective-permute-start | bytes 393224 | tf_op jit(solution)/shard_map/ppermute | solution.py:11
  217.9 18.2 %collective-permute-start.10 = (bf16[512,128]{1,0:T(8,128)(2,1)S(1)}, bf16[512,128]{1,0:T(8,128)(2,1)S(1)}, u32[]{:S(2)}, u32[]{:S(2)}) collective-permute-start(bf16[512,128]{1,0:T(8,128)(2,1)S(1)} %fusion.6), channel_id=1, source_target_pairs={{0,30},{1,31},{2,0},{3,1},{4,2},{5,3},{6,4},{7,5},{8,6},{9,7},{10,... | collective-permute-start | bytes 393224 | tf_op jit(solution)/shard_map/ppermute | solution.py:11
  219.0 17.1 %collective-permute-start.9 = (bf16[512,128]{1,0:T(8,128)(2,1)S(1)}, bf16[512,128]{1,0:T(8,128)(2,1)S(1)}, u32[]{:S(2)}, u32[]{:S(2)}) collective-permute-start(bf16[512,128]{1,0:T(8,128)(2,1)S(1)} %fusion.6), channel_id=1, source_target_pairs={{0,31},{1,0},{2,1},{3,2},{4,3},{5,4},{6,5},{7,6},{8,7},{9,8},{10,9... | collective-permute-start | bytes 393224 | tf_op jit(solution)/shard_map/ppermute | solution.py:11
  222.3 13.7 %collective-permute-start.8 = (bf16[512,128]{1,0:T(8,128)(2,1)S(1)}, bf16[512,128]{1,0:T(8,128)(2,1)S(1)}, u32[]{:S(2)}, u32[]{:S(2)}) collective-permute-start(bf16[512,128]{1,0:T(8,128)(2,1)S(1)} %fusion.6), channel_id=1, source_target_pairs={{0,1},{1,2},{2,3},{3,4},{4,5},{5,6},{6,7},{7,8},{8,9},{9,10},{10,1... | collective-permute-start | bytes 393224 | tf_op jit(solution)/shard_map/ppermute | solution.py:11
  222.3 6.7 %collective-permute-start.6 = (bf16[512,128]{1,0:T(8,128)(2,1)S(1)}, bf16[512,128]{1,0:T(8,128)(2,1)S(1)}, u32[]{:S(2)}, u32[]{:S(2)}) collective-permute-start(bf16[512,128]{1,0:T(8,128)(2,1)S(1)} %fusion.6), channel_id=1, source_target_pairs={{0,3},{1,4},{2,5},{3,6},{4,7},{5,8},{6,9},{7,10},{8,11},{9,12},{10... | collective-permute-start | bytes 393224 | tf_op jit(solution)/shard_map/ppermute | solution.py:11
  223.9 325.1 %reduce-scatter.2.cloned.1.call-start = ((), (), s32[]{:S(2)}) async-start(), calls=%async_computation.2 | async-start | bytes 1179648 | tf_op jit(solution)/shard_map/reduce_scatter | solution.py:99
  229.0 7.0 %collective-permute-start.7 = (bf16[512,128]{1,0:T(8,128)(2,1)S(1)}, bf16[512,128]{1,0:T(8,128)(2,1)S(1)}, u32[]{:S(2)}, u32[]{:S(2)}) collective-permute-start(bf16[512,128]{1,0:T(8,128)(2,1)S(1)} %fusion.6), channel_id=1, source_target_pairs={{0,2},{1,3},{2,4},{3,5},{4,6},{5,7},{6,8},{7,9},{8,10},{9,11},{10,... | collective-permute-start | bytes 393224 | tf_op jit(solution)/shard_map/ppermute | solution.py:11
Sparse Core Ops, SparseCore 0:
  11.2 53.9 all-gather.1
  224.0 245.4 all-reduce.1
  473.4 75.5 reduce-scatter.1
where the time goes:
time: 561 us; the launch traced here: 557 us
  waiting for transfers between devices  189 us (34%)
  other arithmetic  164 us (29%)
  blocking collectives  75.9 us (14%)
  matrix products  55.7 us (10%)
  local copies, waits for them, and re-layouts  42.9 us (8%)
  between operations  14.6 us (3%)
  starting transfers between devices  14.4 us (3%)
    scatter-add x16, other arithmetic, add_block(): jax.ops.segment_sum(products, segment_part, segment_total + 1)  105 us
    reduce_scatter x1, waiting for transfers between devices, on_device(): lax.psum_scatter(column_part.reshape(rep_count * row_count, feat_width).a...  77.9 us
    psum x1, blocking collectives, on_device(): weight_sum, bias_sum = lax.psum((local_weight, local_bias), ('rep', 'blk'))  75.9 us
    dot_general x16, matrix products, add_block(): jnp.einsum(pattern, weights_part, source_tiles[gather_part], preferred_el...  53.5 us
    all_gather x1, waiting for transfers between devices, on_device(): source_rows = lax.all_gather(scaled, 'rep', axis=0, tiled=True)  53.4 us
    add x16, other arithmetic, add_block(): running + jax.ops.segment_sum(products, segment_part, segment_total + 1)[...  46.3 us
    psum x1, waiting for transfers between devices, on_device(): weight_sum, bias_sum = lax.psum((local_weight, local_bias), ('rep', 'blk'))  41.1 us
    gather x16, local copies, waits for them, and re-layouts, add_block(): source_tiles[gather_part]  22.5 us
  transfers between devices with their start and end apart: 15, of which 7 were waited for; matrix products, arithmetic and copies ran while one was open for 24% of the time, Pallas kernels for 0%

commit v1 on v0

--- a/solution.py
+++ b/solution.py
@@ -4,6 +4,11 @@
 from jax.sharding import PartitionSpec as P
 
 REACH = 3
+
+
+def axis_by_axis(x, inner_axis, outer_axis):
+    half = lax.psum(x, inner_axis)
+    return lax.psum(half, outer_axis)
 
 
 def shifted(value, axis, by):
@@ -85,7 +90,7 @@
     ).astype(jnp.bfloat16)
     local_weight = jnp.dot(aggregated.T, pre_grad, preferred_element_type=jnp.float32)
     local_bias = jnp.sum(pre_grad.astype(jnp.float32), axis=0)
-    weight_sum, bias_sum = lax.psum((local_weight, local_bias), ("rep", "blk"))
+    weight_sum, bias_sum = axis_by_axis((local_weight, local_bias), "blk", "rep")
     grad_scale = (row_count * rep_count * blk_count) ** (-0.5)
     scaled_grad = (
         node_norm[:, None] * jnp.dot(pre_grad, weight.T, preferred_element_type=jnp.float32)

time: 561 us -> 632 us (1.13)
  waiting for transfers between devices: 189 us -> 261 us
    psum x1 -> x2, waiting for transfers between devices: 41.1 us -> 197 us  [the longest x1 197 us: axis_by_axis(): half = lax.psum(x, inner_axis)]
    reduce_scatter x1, waiting for transfers between devices: 77.9 us -> 4.42 us  [on_device(): lax.psum_scatter(column_part.reshape(rep_count * row_count, feat_width).a...]
    ppermute x12, waiting for transfers between devices: 16.3 us -> 5.64 us  [shifted(): lax.ppermute(value, axis, [(i, (i + by) % length) for i in range(length)])]
    psum x1 -> x2, blocking collectives: 75.9 us -> 73.9 us  [the longest x1 50 us: axis_by_axis(): half = lax.psum(x, inner_axis)]
  transfers between devices with their start and end apart: 15 -> 16, of which waited for: 7 -> 4; matrix products, arithmetic and copies ran while one was open for 24% -> 21% of each run, Pallas kernels for 0% -> 0%
where the time goes in v1:
time: 632 us; the launch traced here: 627 us
  waiting for transfers between devices  261 us (41%)
  other arithmetic  164 us (26%)
  blocking collectives  73.9 us (12%)
  matrix products  55.6 us (9%)
  local copies, waits for them, and re-layouts  42.8 us (7%)
  between operations  14.7 us (2%)
  starting transfers between devices  14 us (2%)
    psum x1, waiting for transfers between devices, axis_by_axis(): half = lax.psum(x, inner_axis)  197 us
    scatter-add x16, other arithmetic, add_block(): jax.ops.segment_sum(products, segment_part, segment_total + 1)  105 us
    all_gather x1, waiting for transfers between devices, on_device(): source_rows = lax.all_gather(scaled, 'rep', axis=0, tiled=True)  53.4 us
    dot_general x16, matrix products, add_block(): jnp.einsum(pattern, weights_part, source_tiles[gather_part], preferred_el...  53.4 us
    psum x1, blocking collectives, axis_by_axis(): half = lax.psum(x, inner_axis)  50 us
    add x16, other arithmetic, add_block(): running + jax.ops.segment_sum(products, segment_part, segment_total + 1)[...  46.3 us
    psum x1, blocking collectives, axis_by_axis(): return lax.psum(half, outer_axis)  23.9 us
    gather x16, local copies, waits for them, and re-layouts, add_block(): source_tiles[gather_part]  22.5 us
  transfers between devices with their start and end apart: 16, of which 4 were waited for; matrix products, arithmetic and copies ran while one was open for 21% of the time, Pallas kernels for 0%

profile of v1, /device:TPU:32, one launch (start us, length us, event | category | flops | bytes accessed | tf_op | source)
XLA Modules:
  0.0 626.9 jit_solution(8808756606373173404)
XLA Ops:
  11.8 53.4 %all-gather.2.cloned.1.call-done = bf16[4096,128]{1,0:T(8,128)(2,1)} async-done(((bf16[512,128]{1,0:T(8,128)(2,1)}), bf16[4096,128]{1,0:T(8,128)(2,1)}) %all-gather.2.cloned.1.call-update) | async-done | bytes 1048592 | tf_op jit(solution)/shard_map/all_gather | solution.py:71
  65.2 120.4 %while.28 = (s32[]{:T(128)}, f32[28,128,128]{2,1,0:T(8,128)}, s32[320]{0:T(512)S(1)}, bf16[320,128,128]{2,1,0:T(8,128)(2,1)}, s32[320]{0:T(512)S(1)}, /*index=5*...) while((s32[]{:T(128)}, f32[28,128,128]{2,1,0:T(8,128)}, ...), condition=%wide.region_2.3_spmd.clone, body=%wide.region_0.2_spmd.clone.sunk | while | flops 169346176 | bytes 23139612 | solution.py:67
  65.4 2.0 gather_fusion
  67.4 3.3 fusion.44
  70.9 6.5 %scatter_fusion = f32[29,128,128]{2,1,0:T(8,128)S(1)} fusion(f32[29,128,128]{2,1,0:T(8,128)S(1)} %broadcast.127, s32[40]{0:T(128)S(1)} %dynamic_slice.62, f32[40,128,128]{2,1,0:T(8,128)} %fusion.44), kind=kCustom, calls=%fused_computation.2.clone.clone.1 | custom fusion | flops 655360 | bytes 7864480 | tf_op jit(solution)/shard_map/while/body/eval_jaxpr/scatter-add | solution.py:63
  79.1 2.0 gather_fusion
  81.1 3.3 fusion.44
  84.7 6.5 %scatter_fusion = f32[29,128,128]{2,1,0:T(8,128)S(1)} fusion(f32[29,128,128]{2,1,0:T(8,128)S(1)} %broadcast.127, s32[40]{0:T(128)S(1)} %dynamic_slice.62, f32[40,128,128]{2,1,0:T(8,128)} %fusion.44), kind=kCustom, calls=%fused_computation.2.clone.clone.1 | custom fusion | flops 655360 | bytes 7864480 | tf_op jit(solution)/shard_map/while/body/eval_jaxpr/scatter-add | solution.py:63
  91.2 3.0 slice_add_fusion.4
  94.4 2.0 gather_fusion
  96.4 3.3 fusion.44
  99.9 6.5 %scatter_fusion = f32[29,128,128]{2,1,0:T(8,128)S(1)} fusion(f32[29,128,128]{2,1,0:T(8,128)S(1)} %broadcast.127, s32[40]{0:T(128)S(1)} %dynamic_slice.62, f32[40,128,128]{2,1,0:T(8,128)} %fusion.44), kind=kCustom, calls=%fused_computation.2.clone.clone.1 | custom fusion | flops 655360 | bytes 7864480 | tf_op jit(solution)/shard_map/while/body/eval_jaxpr/scatter-add | solution.py:63
  106.5 3.0 slice_add_fusion.4
  111.6 3.3 fusion.44
  115.1 6.5 %scatter_fusion = f32[29,128,128]{2,1,0:T(8,128)S(1)} fusion(f32[29,128,128]{2,1,0:T(8,128)S(1)} %broadcast.127, s32[40]{0:T(128)S(1)} %dynamic_slice.62, f32[40,128,128]{2,1,0:T(8,128)} %fusion.44), kind=kCustom, calls=%fused_computation.2.clone.clone.1 | custom fusion | flops 655360 | bytes 7864480 | tf_op jit(solution)/shard_map/while/body/eval_jaxpr/scatter-add | solution.py:63
  121.7 3.0 slice_add_fusion.4
  124.8 2.0 gather_fusion
  126.8 3.3 fusion.44
  130.4 6.5 %scatter_fusion = f32[29,128,128]{2,1,0:T(8,128)S(1)} fusion(f32[29,128,128]{2,1,0:T(8,128)S(1)} %broadcast.127, s32[40]{0:T(128)S(1)} %dynamic_slice.62, f32[40,128,128]{2,1,0:T(8,128)} %fusion.44), kind=kCustom, calls=%fused_computation.2.clone.clone.1 | custom fusion | flops 655360 | bytes 7864480 | tf_op jit(solution)/shard_map/while/body/eval_jaxpr/scatter-add | solution.py:63
  136.9 3.0 slice_add_fusion.4
  140.1 2.0 gather_fusion
  142.1 3.3 fusion.44
  145.6 6.5 %scatter_fusion = f32[29,128,128]{2,1,0:T(8,128)S(1)} fusion(f32[29,128,128]{2,1,0:T(8,128)S(1)} %broadcast.127, s32[40]{0:T(128)S(1)} %dynamic_slice.62, f32[40,128,128]{2,1,0:T(8,128)} %fusion.44), kind=kCustom, calls=%fused_computation.2.clone.clone.1 | custom fusion | flops 655360 | bytes 7864480 | tf_op jit(solution)/shard_map/while/body/eval_jaxpr/scatter-add | solution.py:63
  152.2 3.0 slice_add_fusion.4
  157.3 3.3 fusion.44
  160.8 6.5 %scatter_fusion = f32[29,128,128]{2,1,0:T(8,128)S(1)} fusion(f32[29,128,128]{2,1,0:T(8,128)S(1)} %broadcast.127, s32[40]{0:T(128)S(1)} %dynamic_slice.62, f32[40,128,128]{2,1,0:T(8,128)} %fusion.44), kind=kCustom, calls=%fused_computation.2.clone.clone.1 | custom fusion | flops 655360 | bytes 7864480 | tf_op jit(solution)/shard_map/while/body/eval_jaxpr/scatter-add | solution.py:63
  167.4 3.0 slice_add_fusion.4
  170.5 2.0 gather_fusion
  172.5 3.3 fusion.44
  176.1 6.5 %scatter_fusion = f32[29,128,128]{2,1,0:T(8,128)S(1)} fusion(f32[29,128,128]{2,1,0:T(8,128)S(1)} %broadcast.127, s32[40]{0:T(128)S(1)} %dynamic_slice.62, f32[40,128,128]{2,1,0:T(8,128)} %fusion.44), kind=kCustom, calls=%fused_computation.2.clone.clone.1 | custom fusion | flops 655360 | bytes 7864480 | tf_op jit(solution)/shard_map/while/body/eval_jaxpr/scatter-add | solution.py:63
  182.6 3.0 slice_add_fusion.4
  189.7 2.6 collective-permute-start.2
  194.2 14.4 %copy.13 = bf16[1,1,320,128,128]{3,4,2,1,0:T(8,128)(2,1)} copy(bf16[1,1,320,128,128]{4,3,2,1,0:T(8,128)(2,1)} %bitcast.61) | data formatting | bytes 20971520 | tf_op args[2]
  214.0 3.7 collective-permute-start.10
  218.2 197.5 %all-reduce.3.cloned.1.call-done = f32[128,256]{1,0:T(8,128)} async-done(((f32[128,256]{1,0:T(8,128)}), f32[128,256]{1,0:T(8,128)}) %all-reduce.3.cloned.1.call-update) | async-done | bytes 131088 | tf_op jit(solution)/shard_map/psum | solution.py:10
  416.6 5.6 collective-permute-done.7
  422.4 113.0 %while.29 = (s32[]{:T(128)}, f32[32,128,128]{2,1,0:T(8,128)}, s32[320]{0:T(512)S(1)}, bf16[320,128,128]{1,2,0:T(8,128)(2,1)}, s32[320]{0:T(512)S(1)}, /*index=5*...) while((s32[]{:T(128)}, f32[32,128,128]{2,1,0:T(8,128)}, ...), condition=%wide.region_5.6_spmd.clone, body=%wide.region_3.5_spmd.clone.sunk | while | flops 169477248 | bytes 24188188 | solution.py:67
  423.4 3.3 fusion.47
  427.0 6.6 %scatter_fusion.1 = f32[33,128,128]{2,1,0:T(8,128)S(1)} fusion(f32[33,128,128]{2,1,0:T(8,128)S(1)} %broadcast.134, s32[40]{0:T(128)S(1)} %dynamic_slice.65, f32[40,128,128]{2,1,0:T(8,128)} %fusion.47), kind=kCustom, calls=%fused_computation.3.clone.clone.1 | custom fusion | flops 655360 | bytes 7864480 | tf_op jit(solution)/shard_map/while/body/eval_jaxpr/scatter-add | solution.py:63
  436.2 3.3 fusion.47
  439.8 6.6 %scatter_fusion.1 = f32[33,128,128]{2,1,0:T(8,128)S(1)} fusion(f32[33,128,128]{2,1,0:T(8,128)S(1)} %broadcast.134, s32[40]{0:T(128)S(1)} %dynamic_slice.65, f32[40,128,128]{2,1,0:T(8,128)} %fusion.47), kind=kCustom, calls=%fused_computation.3.clone.clone.1 | custom fusion | flops 655360 | bytes 7864480 | tf_op jit(solution)/shard_map/while/body/eval_jaxpr/scatter-add | solution.py:63
  446.3 3.2 slice_add_fusion.5
  450.5 3.4 fusion.47
  454.1 6.6 %scatter_fusion.1 = f32[33,128,128]{2,1,0:T(8,128)S(1)} fusion(f32[33,128,128]{2,1,0:T(8,128)S(1)} %broadcast.134, s32[40]{0:T(128)S(1)} %dynamic_slice.65, f32[40,128,128]{2,1,0:T(8,128)} %fusion.47), kind=kCustom, calls=%fused_computation.3.clone.clone.1 | custom fusion | flops 655360 | bytes 7864480 | tf_op jit(solution)/shard_map/while/body/eval_jaxpr/scatter-add | solution.py:63
  460.7 3.2 slice_add_fusion.5
  464.8 3.4 fusion.47
  468.4 6.6 %scatter_fusion.1 = f32[33,128,128]{2,1,0:T(8,128)S(1)} fusion(f32[33,128,128]{2,1,0:T(8,128)S(1)} %broadcast.134, s32[40]{0:T(128)S(1)} %dynamic_slice.65, f32[40,128,128]{2,1,0:T(8,128)} %fusion.47), kind=kCustom, calls=%fused_computation.3.clone.clone.1 | custom fusion | flops 655360 | bytes 7864480 | tf_op jit(solution)/shard_map/while/body/eval_jaxpr/scatter-add | solution.py:63
  475.0 3.2 slice_add_fusion.5
  479.2 3.4 fusion.47
  482.8 6.6 %scatter_fusion.1 = f32[33,128,128]{2,1,0:T(8,128)S(1)} fusion(f32[33,128,128]{2,1,0:T(8,128)S(1)} %broadcast.134, s32[40]{0:T(128)S(1)} %dynamic_slice.65, f32[40,128,128]{2,1,0:T(8,128)} %fusion.47), kind=kCustom, calls=%fused_computation.3.clone.clone.1 | custom fusion | flops 655360 | bytes 7864480 | tf_op jit(solution)/shard_map/while/body/eval_jaxpr/scatter-add | solution.py:63
  489.3 3.2 slice_add_fusion.5
  493.5 3.4 fusion.47
  497.1 6.5 %scatter_fusion.1 = f32[33,128,128]{2,1,0:T(8,128)S(1)} fusion(f32[33,128,128]{2,1,0:T(8,128)S(1)} %broadcast.134, s32[40]{0:T(128)S(1)} %dynamic_slice.65, f32[40,128,128]{2,1,0:T(8,128)} %fusion.47), kind=kCustom, calls=%fused_computation.3.clone.clone.1 | custom fusion | flops 655360 | bytes 7864480 | tf_op jit(solution)/shard_map/while/body/eval_jaxpr/scatter-add | solution.py:63
  503.6 3.2 slice_add_fusion.5
  507.8 3.4 fusion.47
  511.4 6.5 %scatter_fusion.1 = f32[33,128,128]{2,1,0:T(8,128)S(1)} fusion(f32[33,128,128]{2,1,0:T(8,128)S(1)} %broadcast.134, s32[40]{0:T(128)S(1)} %dynamic_slice.65, f32[40,128,128]{2,1,0:T(8,128)} %fusion.47), kind=kCustom, calls=%fused_computation.3.clone.clone.1 | custom fusion | flops 655360 | bytes 7864480 | tf_op jit(solution)/shard_map/while/body/eval_jaxpr/scatter-add | solution.py:63
  517.9 3.2 slice_add_fusion.5
  522.1 3.4 fusion.47
  525.7 6.5 %scatter_fusion.1 = f32[33,128,128]{2,1,0:T(8,128)S(1)} fusion(f32[33,128,128]{2,1,0:T(8,128)S(1)} %broadcast.134, s32[40]{0:T(128)S(1)} %dynamic_slice.65, f32[40,128,128]{2,1,0:T(8,128)} %fusion.47), kind=kCustom, calls=%fused_computation.3.clone.clone.1 | custom fusion | flops 655360 | bytes 7864480 | tf_op jit(solution)/shard_map/while/body/eval_jaxpr/scatter-add | solution.py:63
  532.3 3.2 slice_add_fusion.5
  535.5 2.7 convert_element_type.108
  538.2 50.0 %psum.30 = f32[256]{0:T(256)S(1)} all-reduce(f32[256]{0:T(256)S(1)} %get-tuple-element.296), channel_id=1, replica_groups=mesh['rep'=8,'blk'=32] {'blk'}, use_global_device_ids=true, to_apply=%region_10.11 | all-reduce | flops 256 | bytes 2048 | tf_op jit(solution)/shard_map/psum | solution.py:10
  588.2 23.9 %psum.31 = f32[256]{0:T(256)S(1)} all-reduce(f32[256]{0:T(256)S(1)} %psum.30), channel_id=1, replica_groups=mesh['rep'=8,'blk'=32] {'rep'}, use_global_device_ids=true, to_apply=%region_11.12 | all-reduce | flops 256 | bytes 2048 | tf_op jit(solution)/shard_map/psum | solution.py:11
  614.3 4.4 reduce-scatter.2.cloned.1.call-done
  (139 shorter events, 40.1 us)
Async XLA Ops:
  7.2 202.7 %copy-start = (bf16[128,256]{1,0:T(8,128)(2,1)S(1)}, bf16[128,256]{1,0:T(8,128)(2,1)}, u32[]{:S(2)}) copy-start(bf16[128,256]{1,0:T(8,128)(2,1)} %param.19) | copy-start | bytes 196612
  7.2 58.0 %all-gather.2.cloned.1.call-start = ((), (), s32[]{:S(2)}) async-start(), calls=%async_computation.1 | async-start | bytes 1179648 | tf_op jit(solution)/shard_map/all_gather | solution.py:71
  9.6 406.0 %all-reduce.3.cloned.1.call-start = ((), (), s32[]{:S(2)}) async-start(), calls=%async_computation.3 | async-start | bytes 262144 | tf_op jit(solution)/shard_map/psum | solution.py:10
  187.3 5.0 collective-permute-start.5
  187.4 22.2 %collective-permute-start = (bf16[512,128]{1,0:T(8,128)(2,1)S(1)}, bf16[512,128]{1,0:T(8,128)(2,1)S(1)}, u32[]{:S(2)}, u32[]{:S(2)}) collective-permute-start(bf16[512,128]{1,0:T(8,128)(2,1)S(1)} %bitcast.68), channel_id=1, source_target_pairs={{0,29},{1,30},{2,31},{3,0},{4,1},{5,2},{6,3},{7,4},{8,5},{9,6},{10... | collective-permute-start | bytes 393224 | tf_op jit(solution)/shard_map/ppermute | solution.py:16
  189.1 20.5 %collective-permute-start.4 = (bf16[512,128]{1,0:T(8,128)(2,1)S(1)}, bf16[512,128]{1,0:T(8,128)(2,1)S(1)}, u32[]{:S(2)}, u32[]{:S(2)}) collective-permute-start(bf16[512,128]{1,0:T(8,128)(2,1)S(1)} %bitcast.67), channel_id=1, source_target_pairs={{0,2},{1,3},{2,4},{3,5},{4,6},{5,7},{6,8},{7,9},{8,10},{9,11},{10,... | collective-permute-start | bytes 393224 | tf_op jit(solution)/shard_map/ppermute | solution.py:16
  189.7 19.9 %collective-permute-start.3 = (bf16[512,128]{1,0:T(8,128)(2,1)S(1)}, bf16[512,128]{1,0:T(8,128)(2,1)S(1)}, u32[]{:S(2)}, u32[]{:S(2)}) collective-permute-start(bf16[512,128]{1,0:T(8,128)(2,1)S(1)} %bitcast.66), channel_id=1, source_target_pairs={{0,1},{1,2},{2,3},{3,4},{4,5},{5,6},{6,7},{7,8},{8,9},{9,10},{10,1... | collective-permute-start | bytes 393224 | tf_op jit(solution)/shard_map/ppermute | solution.py:16
  189.7 19.9 %collective-permute-start.2 = (bf16[512,128]{1,0:T(8,128)(2,1)S(1)}, bf16[512,128]{1,0:T(8,128)(2,1)S(1)}, u32[]{:S(2)}, u32[]{:S(2)}) collective-permute-start(bf16[512,128]{1,0:T(8,128)(2,1)S(1)} %bitcast.65), channel_id=1, source_target_pairs={{0,31},{1,0},{2,1},{3,2},{4,3},{5,4},{6,5},{7,6},{8,7},{9,8},{10,9... | collective-permute-start | bytes 393224 | tf_op jit(solution)/shard_map/ppermute | solution.py:16
  192.3 17.3 %collective-permute-start.1 = (bf16[512,128]{1,0:T(8,128)(2,1)S(1)}, bf16[512,128]{1,0:T(8,128)(2,1)S(1)}, u32[]{:S(2)}, u32[]{:S(2)}) collective-permute-start(bf16[512,128]{1,0:T(8,128)(2,1)S(1)} %bitcast.64), channel_id=1, source_target_pairs={{0,30},{1,31},{2,0},{3,1},{4,2},{5,3},{6,4},{7,5},{8,6},{9,7},{10,... | collective-permute-start | bytes 393224 | tf_op jit(solution)/shard_map/ppermute | solution.py:16
  194.2 15.4 %copy-start.1 = (bf16[512,128]{1,0:T(8,128)(2,1)S(1)}, bf16[512,128]{1,0:T(8,128)(2,1)}, u32[]{:S(2)}) copy-start(bf16[512,128]{1,0:T(8,128)(2,1)} %param.13) | copy-start | bytes 393220
  194.2 15.6 %copy-start.2 = (bf16[512,256]{1,0:T(8,128)(2,1)S(1)}, bf16[512,256]{1,0:T(8,128)(2,1)}, u32[]{:S(2)}) copy-start(bf16[512,256]{1,0:T(8,128)(2,1)} %param.21) | copy-start | bytes 786436
  194.2 15.6 %copy-start.3 = (f32[256]{0:T(256)S(1)}, f32[256]{0:T(256)}, u32[]{:S(2)}) copy-start(f32[256]{0:T(256)} %param.20) | copy-start | bytes 3076
  212.1 400.6 %all-reduce.5.cloned.1.call-start = ((), (), s32[]{:S(2)}) async-start(), calls=%async_computation.4 | async-start | bytes 262144 | tf_op jit(solution)/shard_map/psum | solution.py:11
  212.2 203.6 %collective-permute-start.6 = (bf16[512,128]{1,0:T(8,128)(2,1)S(1)}, bf16[512,128]{1,0:T(8,128)(2,1)S(1)}, u32[]{:S(2)}, u32[]{:S(2)}) collective-permute-start(bf16[512,128]{1,0:T(8,128)(2,1)S(1)} %fusion.6), channel_id=1, source_target_pairs={{0,3},{1,4},{2,5},{3,6},{4,7},{5,8},{6,9},{7,10},{8,11},{9,12},{10... | collective-permute-start | bytes 393224 | tf_op jit(solution)/shard_map/ppermute | solution.py:16
  212.3 210.2 %collective-permute-start.11 = (bf16[512,128]{1,0:T(8,128)(2,1)S(1)}, bf16[512,128]{1,0:T(8,128)(2,1)S(1)}, u32[]{:S(2)}, u32[]{:S(2)}) collective-permute-start(bf16[512,128]{1,0:T(8,128)(2,1)S(1)} %fusion.6), channel_id=1, source_target_pairs={{0,29},{1,30},{2,31},{3,0},{4,1},{5,2},{6,3},{7,4},{8,5},{9,6},{10... | collective-permute-start | bytes 393224 | tf_op jit(solution)/shard_map/ppermute | solution.py:16
  214.0 208.4 %collective-permute-start.10 = (bf16[512,128]{1,0:T(8,128)(2,1)S(1)}, bf16[512,128]{1,0:T(8,128)(2,1)S(1)}, u32[]{:S(2)}, u32[]{:S(2)}) collective-permute-start(bf16[512,128]{1,0:T(8,128)(2,1)S(1)} %fusion.6), channel_id=1, source_target_pairs={{0,30},{1,31},{2,0},{3,1},{4,2},{5,3},{6,4},{7,5},{8,6},{9,7},{10,... | collective-permute-start | bytes 393224 | tf_op jit(solution)/shard_map/ppermute | solution.py:16
  217.7 204.6 %collective-permute-start.9 = (bf16[512,128]{1,0:T(8,128)(2,1)S(1)}, bf16[512,128]{1,0:T(8,128)(2,1)S(1)}, u32[]{:S(2)}, u32[]{:S(2)}) collective-permute-start(bf16[512,128]{1,0:T(8,128)(2,1)S(1)} %fusion.6), channel_id=1, source_target_pairs={{0,31},{1,0},{2,1},{3,2},{4,3},{5,4},{6,5},{7,6},{8,7},{9,8},{10,9... | collective-permute-start | bytes 393224 | tf_op jit(solution)/shard_map/ppermute | solution.py:16
  218.2 204.0 %collective-permute-start.8 = (bf16[512,128]{1,0:T(8,128)(2,1)S(1)}, bf16[512,128]{1,0:T(8,128)(2,1)S(1)}, u32[]{:S(2)}, u32[]{:S(2)}) collective-permute-start(bf16[512,128]{1,0:T(8,128)(2,1)S(1)} %fusion.6), channel_id=1, source_target_pairs={{0,1},{1,2},{2,3},{3,4},{4,5},{5,6},{6,7},{7,8},{8,9},{9,10},{10,1... | collective-permute-start | bytes 393224 | tf_op jit(solution)/shard_map/ppermute | solution.py:16
  415.7 203.0 %reduce-scatter.2.cloned.1.call-start = ((), (), s32[]{:S(2)}) async-start(), calls=%async_computation.2 | async-start | bytes 1179648 | tf_op jit(solution)/shard_map/reduce_scatter | solution.py:104
  415.8 6.5 %collective-permute-start.7 = (bf16[512,128]{1,0:T(8,128)(2,1)S(1)}, bf16[512,128]{1,0:T(8,128)(2,1)S(1)}, u32[]{:S(2)}, u32[]{:S(2)}) collective-permute-start(bf16[512,128]{1,0:T(8,128)(2,1)S(1)} %fusion.6), channel_id=1, source_target_pairs={{0,2},{1,3},{2,4},{3,5},{4,6},{5,7},{6,8},{7,9},{8,10},{9,11},{10,... | collective-permute-start | bytes 393224 | tf_op jit(solution)/shard_map/ppermute | solution.py:16
Sparse Core Ops, SparseCore 0:
  11.2 53.9 all-gather.1
  212.2 203.4 all-reduce.2
  418.3 91.4 all-reduce.4
  538.3 80.3 reduce-scatter.1
